TPU v7x, 32 devices: a whole 2x2x4 slice. The times are simulated.
32 devices in a mesh: groups: 2 (over x), corpus: 16 (over z, y, core).
Axes of the slice: x: 2, y: 2, z: 4, core: 2. Of those that a mesh axis runs over, the one named last changes fastest.
Arguments:
- queries: bfloat16 [1792, 32, 128], P(('groups', 'corpus')), parts along dimension 0, may hold values from -6 to 6
- passages: bfloat16 [4096, 128, 128], P(('groups', 'corpus')), parts along dimension 0, may hold values from -0.5 to 0.5
- lengths: int32 [4096], P(('groups', 'corpus')), parts along dimension 0, may hold values from 8 to 128
- candidates: int32 [32, 128], P(('groups', 'corpus')), parts along dimension 0, may hold values from 0 to 2047, as said below
Outputs:
- scores: float32 [1792, 128], P(('groups', 'corpus')), parts along dimension 0
- best_scores: float32 [1792, 100], P(('groups', 'corpus')), parts along dimension 0
There are 2 independent parts, one for each index of `groups`. A program takes and returns all parts, laid end to end along the dimension named above; each array names one. Nothing has to cross between parts.
Inputs may be any that keep to these rules, and one draw needn't show every extreme that they name: Row b lists the candidates of queries b * 56 to (b + 1) * 56 - 1. Passage p is held by owner p // 128. In every row at most 12 entries share an owner, and in every row some owner holds exactly 12 of them. Entries may repeat. `lengths`: rows of a tile at or past its length are padding.
All inputs are finite; a program needn't handle non-finite values.
Results may differ from a plain program's by a relative error of at most 0.0003.
Values may be sent and summed in bfloat16 or wider, within the bound.
A program may use at most 128 MiB of HBM per device.

v0:
```python
import functools

import jax
import jax.numpy as jnp
from jax import lax
from jax.experimental import pallas as pl
from jax.experimental.pallas import tpu as pltpu
from jax.sharding import PartitionSpec as P

TOPK = 100
MESH = pl.DeviceIdType.MESH


def pick_tile(rows, tok):
    tile = 256
    while rows % tile or tile % tok:
        tile //= 2
    return tile


def sort_down(x):
    count, width = x.shape
    index = lax.broadcasted_iota(jnp.int32, (count // 8, 8, width), 0) * 8
    index = index + lax.broadcasted_iota(jnp.int32, (count // 8, 8, width), 1)
    x = x.reshape(count // 8, 8, width)
    size = 2
    while size <= count:
        gap = size // 2
        falling = (index // size) % 2 == 0
        while gap >= 1:
            low = (index // gap) % 2 == 0
            if gap >= 8:
                hop = gap // 8
                y = x.reshape(count // (2 * gap), 2, hop, 8, width)
                y = jnp.concatenate([y[:, 1:], y[:, :1]], axis=1)
                other = y.reshape(x.shape)
            else:
                other = jnp.where(low, pltpu.roll(x, 8 - gap, 1), pltpu.roll(x, gap, 1))
            x = jnp.where(low == falling, jnp.maximum(x, other), jnp.minimum(x, other))
            gap //= 2
        size *= 2
    return x.reshape(count, width)


def split3(x):
    high = x.astype(jnp.bfloat16)
    rest = x - high.astype(jnp.float32)
    mid = rest.astype(jnp.bfloat16)
    low = (rest - mid.astype(jnp.float32)).astype(jnp.bfloat16)
    return high, mid, low


def kernel(cfg, cand_ref, len_ref, q_hbm, p_hbm, out_ref, place_ref, qall, pas, cand_all,
           wanted_v, wanted_s, place, fold, send_buf, got, q_send, q_recv,
           sib_send, sib_recv, id_send, id_recv, sc_send, sc_recv, loc_sem):
    n, ways, cap, per_owner, tile_rows, rows, feature, tok, col = cfg
    chips = n // 2
    half = chips // 2
    depth = chips // ways
    units = rows // col
    cut = (units + 1) // 2
    spans = ((0, cut), (cut, units))
    ends = tuple(((lo, (lo + hi + 1) // 2), ((lo + hi + 1) // 2, hi)) for lo, hi in spans)
    me = lax.axis_index("corpus")
    core = lax.rem(me, 2)
    chip = me // 2
    if ways == 2:
        zz, yy = chip // 2, lax.rem(chip, 2)
        pos = (1 - yy) * zz + yy * (2 * depth - 1 - zz)
    else:
        pos = chip

    def at(p, c):
        p = lax.rem(p + 2 * chips, chips)
        if ways == 2:
            far = p // depth
            p = (1 - far) * (2 * p) + far * ((2 * depth - 1 - p) * 2 + 1)
        return p * 2 + c

    sib = at(pos, 1 - core)
    right, left = at(pos + 1, core), at(pos - 1, core)
    toward = (right, left)

    def origin(d, s, c):
        return at(pos - s if d == 0 else pos + s, c)

    def piece(b, d, s, k):
        lo, hi = ends[d][k] if s == half else spans[k]
        return qall.at[b, pl.ds(lo * col, (hi - lo) * col), :]

    def hop(d, s, k):
        b = origin(d, s - 1, core)
        return pltpu.make_async_remote_copy(
            src_ref=piece(b, d, s, k), dst_ref=piece(b, d, s, k),
            send_sem=q_send.at[d, s, k], recv_sem=q_recv.at[d, s, k],
            device_id={"corpus": toward[d]}, device_id_type=MESH)

    def hop_in(d, s, k):
        b = origin(d, s, core)
        return pltpu.make_async_remote_copy(
            src_ref=piece(b, d, s, k), dst_ref=piece(b, d, s, k),
            send_sem=q_send.at[d, s, k], recv_sem=q_recv.at[d, s, k],
            device_id={"corpus": toward[d]}, device_id_type=MESH)

    def share(d, s, k, c):
        b = origin(d, s, c)
        return pltpu.make_async_remote_copy(
            src_ref=piece(b, d, s, k), dst_ref=piece(b, d, s, k),
            send_sem=sib_send.at[d, s, k], recv_sem=sib_recv.at[d, s, k],
            device_id={"corpus": sib}, device_id_type=MESH)

    def id_copy(o):
        peer = lax.rem(me + o, n)
        return pltpu.make_async_remote_copy(
            src_ref=cand_all.at[me], dst_ref=cand_all.at[me],
            send_sem=id_send.at[o], recv_sem=id_recv.at[me],
            device_id={"corpus": peer}, device_id_type=MESH)

    def id_in(o):
        peer = lax.rem(me + o, n)
        return pltpu.make_async_remote_copy(
            src_ref=cand_all.at[peer], dst_ref=cand_all.at[peer],
            send_sem=id_send.at[o], recv_sem=id_recv.at[peer],
            device_id={"corpus": peer}, device_id_type=MESH)

    def score_copy(b):
        return pltpu.make_async_remote_copy(
            src_ref=send_buf.at[b], dst_ref=got.at[me],
            send_sem=sc_send.at[b], recv_sem=sc_recv.at[me],
            device_id={"corpus": b}, device_id_type=MESH)

    def score_in(o):
        peer = lax.rem(me + o, n)
        return pltpu.make_async_remote_copy(
            src_ref=send_buf.at[peer], dst_ref=got.at[peer],
            send_sem=sc_send.at[peer], recv_sem=sc_recv.at[peer],
            device_id={"corpus": peer}, device_id_type=MESH)

    q_load = pltpu.make_async_copy(q_hbm, qall.at[me], loc_sem.at[0])
    c_load = pltpu.make_async_copy(cand_ref, cand_all.at[me], loc_sem.at[2])
    p_load = pltpu.make_async_copy(p_hbm, pas, loc_sem.at[1])
    c_load.start()
    q_load.start()
    p_load.start()

    barrier = pltpu.get_barrier_semaphore()

    def greet(o, _):
        pl.semaphore_signal(barrier, inc=1, device_id={"corpus": lax.rem(me + o, n)},
                            device_id_type=MESH)
        return 0

    lax.fori_loop(1, n, greet, 0)
    c_load.wait()
    q_load.wait()
    pl.semaphore_wait(barrier, n - 1)

    def each(first, fn):
        def body(o, _):
            fn(o)
            return 0
        lax.fori_loop(first, n, body, 0)

    each(1, lambda o: id_copy(o).start())
    for k in range(2):
        for d in range(2):
            hop(d, 1, k).start()
        share(0, 0, k, core).start()
    row_at = lax.broadcasted_iota(jnp.int32, (rows, 128), 0) // tok
    lane_at = lax.broadcasted_iota(jnp.int32, (rows, 128), 1)
    fold[...] = jnp.where(row_at == lane_at, 1.0, 0.0).astype(fold.dtype)
    slots = send_buf.shape[1]
    number = cand_ref.shape[1]
    mine_row = lax.div(cand_ref[...], per_owner).astype(jnp.float32)
    across = jnp.broadcast_to(mine_row, (number, number))
    down = across.T
    r_at = lax.broadcasted_iota(jnp.int32, (number, number), 0)
    c_at = lax.broadcasted_iota(jnp.int32, (number, number), 1)
    ahead = jnp.where((across == down) & (c_at < r_at), 1.0, 0.0)
    slot = down[:, :1] * float(slots) + jnp.sum(ahead, axis=1, keepdims=True)
    slot_at = lax.broadcasted_iota(jnp.int32, place.shape, 1).astype(jnp.float32)
    place[...] = jnp.where(slot_at == slot, 1.0, 0.0).astype(place.dtype)
    in_tile = lax.broadcasted_iota(jnp.int32, (tile_rows, feature), 0)
    p_load.wait()

    def fill(i, _):
        for j in range(4):
            p = i * 4 + j
            tile = pas[p].astype(jnp.float32)
            tile = jnp.where(in_tile < len_ref[p], tile, tile[0:1, :])
            pas[p] = tile.astype(pas.dtype)
        return 0

    lax.fori_loop(0, per_owner // 4, fill, 0)
    each(1, lambda o: id_in(o).wait_recv())

    ids = cand_all[...].reshape(n, cand_all.shape[2])
    owner = lax.div(ids, per_owner)
    local = ids - owner * per_owner
    mine = owner == me
    before = jnp.where(r_at < c_at, 1.0, 0.0).astype(jnp.bfloat16)
    rank = jnp.dot(jnp.where(mine, 1.0, 0.0).astype(jnp.bfloat16), before,
                   preferred_element_type=jnp.float32)
    lane = lax.broadcasted_iota(jnp.int32, (n, number), 1)
    wanted = jnp.zeros((n, number), jnp.int32)
    for s in range(cap):
        hit = mine & (rank == float(s))
        found = jnp.max(jnp.where(hit, local, 0), axis=1, keepdims=True)
        wanted = jnp.where(lane == s, found, wanted)
    wanted_v[...] = wanted
    w_load = pltpu.make_async_copy(wanted_v, wanted_s, loc_sem.at[3])
    w_load.start()
    w_load.wait()

    def compute(b, lo, hi):
        chosen = [wanted_s[b, s] for s in range(cap)]
        pieces = []
        for u in range(lo, hi):
            qs = qall[b, pl.ds(u * col, col), :]
            near = []
            for s in range(cap):
                sim = lax.dot_general(pas[chosen[s]], qs, (((1,), (1,)), ((), ())),
                                      preferred_element_type=jnp.float32)
                near.append(jnp.max(sim, axis=0, keepdims=True))
            if cap < slots:
                near.append(jnp.zeros((slots - cap, col), jnp.float32))
            near = jnp.concatenate(near, axis=0)
            high = near.astype(jnp.bfloat16).astype(jnp.float32)
            pieces.append(jnp.concatenate([high, near - high], axis=0).astype(jnp.bfloat16))
        part = jnp.dot(jnp.concatenate(pieces, axis=1), fold[pl.ds(lo * col, (hi - lo) * col), :],
                       preferred_element_type=jnp.float32)
        return (part[:slots] + part[slots:]) / float(tok)

    for k in range(2):
        share(0, 0, k, 1 - core).wait_recv()

    def near_body(j, _):
        b = at(pos, lax.rem(core + j, 2))
        send_buf[b] = compute(b, *spans[0]) + compute(b, *spans[1])

        @pl.when(j == 1)
        def _():
            score_copy(b).start()
        return 0

    lax.fori_loop(0, 2, near_body, 0)
    got[me] = send_buf[me]

    for s in range(1, half):
        for k in range(2):
            for d in range(2):
                hop_in(d, s, k).wait_recv()
                if s + 1 < half:
                    hop(d, s + 1, k).start()
                elif k == d:
                    for m in range(2):
                        hop(d, half, m).start()
                share(d, s, k, core).start()

            def ring_body(j, _, s=s, k=k):
                @pl.when(j == 1)
                def _():
                    for d in range(2):
                        share(d, s, k, 1 - core).wait_recv()
                blocks = [origin(d, s, lax.rem(core + j, 2)) for d in range(2)]
                found = [compute(b, *spans[k]) for b in blocks]
                for b, part in zip(blocks, found):
                    send_buf[b] = part if k == 0 else send_buf[b] + part
                if k == 1:
                    for b in blocks:
                        score_copy(b).start()
                return 0

            lax.fori_loop(0, 2, ring_body, 0)
    for m in range(2):
        for d in range(2):
            hop_in(d, half, m).wait_recv()
            share(d, half, m, core).start()

        def last_body(j, _, m=m):
            b = at(pos + half, lax.rem(core + j, 2))

            @pl.when(j == 1)
            def _():
                for d in range(2):
                    share(d, half, m, 1 - core).wait_recv()
            part = compute(b, *ends[0][m]) + compute(b, *ends[1][m])
            send_buf[b] = part if m == 0 else send_buf[b] + part
            if m == 1:
                score_copy(b).start()
            return 0

        lax.fori_loop(0, 2, last_body, 0)

    for k in range(2):
        share(0, 0, k, core).wait_send()
        for d in range(2):
            for s in range(1, half + 1):
                hop(d, s, k).wait_send()
                share(d, s, k, core).wait_send()
    each(1, lambda o: id_copy(o).wait_send())
    each(1, lambda o: score_copy(lax.rem(me + o, n)).wait_send())
    each(1, lambda o: score_in(o).wait_recv())
    out_ref[...] = got[...].reshape(out_ref.shape)
    place_ref[...] = place[...]


def finish(got_ref, place_ref, out_ref, best_ref):
    spread = None
    for part in split3(got_ref[...]):
        term = jnp.dot(place_ref[...], part, preferred_element_type=jnp.float32)
        spread = term if spread is None else spread + term
    queries = out_ref.shape[0]
    out_ref[...] = spread.T[:queries]
    best_ref[...] = sort_down(spread).T[:queries, :best_ref.shape[1]]


def local(ways, queries, passages, lengths, candidates):
    n = lax.axis_size("corpus")
    per_owner, tile_rows, feature = passages.shape
    per_device, tok = queries.shape[0], queries.shape[1]
    number = candidates.shape[1]
    rows = per_device * tok
    cap = max(2, 3 * number // (2 * n))
    slots = -(-cap // 8) * 8
    col = pick_tile(rows, tok)
    half = n // 4
    cfg = (n, ways, cap, per_owner, tile_rows, rows, feature, tok, col)
    got, place = pl.pallas_call(
        functools.partial(kernel, cfg),
        out_shape=(
            jax.ShapeDtypeStruct((n * slots, 128), jnp.float32),
            jax.ShapeDtypeStruct((number, n * slots), jnp.bfloat16),
        ),
        in_specs=[
            pl.BlockSpec(memory_space=pltpu.VMEM),
            pl.BlockSpec(memory_space=pltpu.SMEM),
            pl.BlockSpec(memory_space=pl.ANY),
            pl.BlockSpec(memory_space=pl.ANY),
        ],
        out_specs=(
            pl.BlockSpec(memory_space=pltpu.VMEM),
            pl.BlockSpec(memory_space=pltpu.VMEM),
        ),
        scratch_shapes=[
            pltpu.VMEM((n, rows, feature), queries.dtype),
            pltpu.VMEM(passages.shape, passages.dtype),
            pltpu.VMEM((n, 1, number), jnp.int32),
            pltpu.VMEM((n, number), jnp.int32),
            pltpu.SMEM((n, number), jnp.int32),
            pltpu.VMEM((number, n * slots), jnp.bfloat16),
            pltpu.VMEM((rows, 128), jnp.bfloat16),
            pltpu.VMEM((n, slots, 128), jnp.float32),
            pltpu.VMEM((n, slots, 128), jnp.float32),
            pltpu.SemaphoreType.DMA((2, half + 1, 2)),
            pltpu.SemaphoreType.DMA((2, half + 1, 2)),
            pltpu.SemaphoreType.DMA((2, half + 1, 2)),
            pltpu.SemaphoreType.DMA((2, half + 1, 2)),
            pltpu.SemaphoreType.DMA((n,)),
            pltpu.SemaphoreType.DMA((n,)),
            pltpu.SemaphoreType.DMA((n,)),
            pltpu.SemaphoreType.DMA((n,)),
            pltpu.SemaphoreType.DMA((4,)),
        ],
        compiler_params=pltpu.CompilerParams(
            collective_id=0, has_side_effects=True, vmem_limit_bytes=60 * 2**20),
    )(candidates, lengths, queries.reshape(rows, feature), passages)
    return pl.pallas_call(
        finish,
        out_shape=(
            jax.ShapeDtypeStruct((per_device, number), jnp.float32),
            jax.ShapeDtypeStruct((per_device, TOPK), jnp.float32),
        ),
        in_specs=[pl.BlockSpec(memory_space=pltpu.VMEM)] * 2,
        out_specs=(pl.BlockSpec(memory_space=pltpu.VMEM), pl.BlockSpec(memory_space=pltpu.VMEM)),
    )(got, place)


def solution(mesh):
    ways = 2 if mesh.shape["groups"] == 2 else 1
    return jax.shard_map(
        functools.partial(local, ways),
        mesh=mesh,
        in_specs=(
            P(("groups", "corpus"), None, None),
            P(("groups", "corpus"), None, None),
            P(("groups", "corpus")),
            P(("groups", "corpus"), None),
        ),
        out_specs=(P(("groups", "corpus"), None), P(("groups", "corpus"), None)),
        check_vma=False,
    )
```

profile of v0, /device:TPU:0, one launch (start us, length us, event | category | flops | bytes accessed | tf_op | source)
XLA Modules:
  0.0 56.7 jit_solution(8194697814783191232)
XLA Ops:
  0.6 53.9 %shard_map.59 = (f32[256,128]{1,0:T(8,128)}, bf16[128,256]{1,0:T(8,128)(2,1)}) custom-call(s32[1,128]{1,0:T(1,128)} %cand_ref.1, s32[128]{0:T(128)} %len_ref.1, bf16[1792,128]{1,0:T(8,128)(2,1)} %bitcast.1, bf16[128,128,128]{2,1,0:T(8,128)(2,1)} %p_hbm.1), custom_call_target="tpu_custom_call" | custom-call | tf_op jit(solution)/shard_map/pallas_call | solution.py:329
  54.6 2.1 %shard_map.60 = (f32[56,128]{1,0:T(8,128)}, f32[56,100]{1,0:T(8,128)}) custom-call(f32[256,128]{1,0:T(8,128)} %get-tuple-element.4.got_ref, bf16[128,256]{1,0:T(8,128)(2,1)} %get-tuple-element.5.place_ref), custom_call_target="tpu_custom_call" | custom-call | tf_op jit(solution)/shard_map/pallas_call | solution.py:368
where the time goes:
time: 56.8 us; the launch traced here: 56.7 us
  Pallas kernels  56 us (99%)
  between operations  0.64 us (1%)
    pallas_call x1, Pallas kernels, local(): pl.pallas_call(functools.partial(kernel, cfg), out_shape=(jax.ShapeDtypeS...  53.9 us
    pallas_call x1, Pallas kernels, local(): pl.pallas_call(finish, out_shape=(jax.ShapeDtypeStruct((per_device, numbe...  2.08 us

commit v1 on v0

v1 whole, which is shorter than its diff:
```python
import functools

import jax
import jax.numpy as jnp
from jax import lax
from jax.experimental import pallas as pl
from jax.experimental.pallas import tpu as pltpu
from jax.sharding import PartitionSpec as P

TOPK = 100
MESH = pl.DeviceIdType.MESH


def pick_tile(rows, tok):
    tile = 256
    while rows % tile or tile % tok:
        tile //= 2
    return tile


def sort_down(x):
    count, width = x.shape
    index = lax.broadcasted_iota(jnp.int32, (count // 8, 8, width), 0) * 8
    index = index + lax.broadcasted_iota(jnp.int32, (count // 8, 8, width), 1)
    x = x.reshape(count // 8, 8, width)
    size = 2
    while size <= count:
        gap = size // 2
        falling = (index // size) % 2 == 0
        while gap >= 1:
            low = (index // gap) % 2 == 0
            if gap >= 8:
                hop = gap // 8
                y = x.reshape(count // (2 * gap), 2, hop, 8, width)
                y = jnp.concatenate([y[:, 1:], y[:, :1]], axis=1)
                other = y.reshape(x.shape)
            else:
                other = jnp.where(low, pltpu.roll(x, 8 - gap, 1), pltpu.roll(x, gap, 1))
            x = jnp.where(low == falling, jnp.maximum(x, other), jnp.minimum(x, other))
            gap //= 2
        size *= 2
    return x.reshape(count, width)


def split3(x):
    high = x.astype(jnp.bfloat16)
    rest = x - high.astype(jnp.float32)
    mid = rest.astype(jnp.bfloat16)
    low = (rest - mid.astype(jnp.float32)).astype(jnp.bfloat16)
    return high, mid, low


def kernel(cfg, cand_hbm, len_hbm, q_hbm, p_hbm, out_ref, place_ref, qall, pas, cand_v, len_s,
           table, wanted, place, fold, stage, send_buf, got, q_send, q_recv, sib_send, sib_recv,
           end_send, end_recv, near_send, near_recv, tail_send, tail_recv, t_send, t_recv,
           tsib_send, tsib_recv, sm_sem, sc_send, sc_recv, loc_sem):
    n, ways, cap, per_owner, tile_rows, rows, feature, tok, col = cfg
    chips = n // 2
    half = chips // 2
    depth = chips // ways
    units = rows // col
    cut = (units + 1) // 2
    spans = []
    for lo, hi in ((0, cut), (cut, units)):
        mid = (lo + hi + 1) // 2
        spans += [(a, b) for a, b in ((lo, mid), (mid, hi)) if b > a]
    pieces = len(spans)
    slots = send_buf.shape[1]
    number = cand_hbm.shape[1]
    me = lax.axis_index("corpus")
    core = lax.rem(me, 2)
    chip = me // 2
    if ways == 2:
        zz, yy = chip // 2, lax.rem(chip, 2)
        pos = (1 - yy) * zz + yy * (2 * depth - 1 - zz)
    else:
        pos = chip

    def at(p, c):
        p = lax.rem(p + 2 * chips, chips)
        if ways == 2:
            far = p // depth
            p = (1 - far) * (2 * p) + far * ((2 * depth - 1 - p) * 2 + 1)
        return p * 2 + c

    sib = at(pos, 1 - core)
    toward = (at(pos + 1, core), at(pos - 1, core))

    def origin(d, s, c):
        return at(pos - s if d == 0 else pos + s, c)

    def remote(src, dst, send, recv, peer):
        return pltpu.make_async_remote_copy(
            src_ref=src, dst_ref=dst, send_sem=send, recv_sem=recv,
            device_id={"corpus": peer}, device_id_type=MESH)

    def span_of(lo, hi):
        return pl.ds(lo * col, (hi - lo) * col)

    def first(d, k):
        cut_k = span_of(*spans[k])
        return remote(q_hbm.at[cut_k, :], qall.at[me, cut_k, :],
                      q_send.at[d, 1, k], q_recv.at[d, 1, k], toward[d])

    def hop(d, s, k, b):
        piece = qall.at[b, span_of(*spans[k]), :]
        return remote(piece, piece, q_send.at[d, s, k], q_recv.at[d, s, k], toward[d])

    def share(d, s, k, b):
        piece = qall.at[b, span_of(*spans[k]), :]
        return remote(piece, piece, sib_send.at[d, s, k], sib_recv.at[d, s, k], sib)

    def near_out(k):
        cut_k = span_of(*spans[k])
        return remote(q_hbm.at[cut_k, :], qall.at[me, cut_k, :],
                      near_send.at[k], near_recv.at[k], sib)

    def near_in(k):
        piece = qall.at[sib, span_of(*spans[k]), :]
        return remote(piece, piece, near_send.at[k], near_recv.at[k], sib)

    def end_hop(e, u, b):
        d = lax.rem(e + core, 2)
        piece = qall.at[b, span_of(u, u + 1), :]
        return remote(piece, piece, end_send.at[u], end_recv.at[u], at(pos + 1 - 2 * d, core))

    def end_share(u, b):
        piece = qall.at[b, span_of(u, u + 1), :]
        return remote(piece, piece, tail_send.at[u], tail_recv.at[u], sib)

    def table_hop(d, s, b):
        return remote(table.at[d, b], table.at[d, b], t_send.at[d, s], t_recv.at[d, s], toward[d])

    def table_share(d, s, b):
        return remote(table.at[d, b], table.at[d, b], tsib_send.at[d, s], tsib_recv.at[d, s], sib)

    my_row = me * slots // 128
    my_lane = lax.rem(me * slots, 128)

    def to_scalar(d, b, who):
        return pltpu.make_async_copy(table.at[d, b, pl.ds(my_row, 1), :],
                                     wanted.at[d, pl.ds(b, 1), :], sm_sem.at[who, d])

    def score_copy(b):
        return remote(send_buf.at[b], got.at[me], sc_send.at[b], sc_recv.at[me], b)

    def score_in(b):
        return remote(send_buf.at[b], got.at[b], sc_send.at[b], sc_recv.at[b], b)

    barrier = pltpu.get_barrier_semaphore()
    for peer in (*toward, sib):
        pl.semaphore_signal(barrier, inc=1, device_id={"corpus": peer}, device_id_type=MESH)
    c_load = pltpu.make_async_copy(cand_hbm, cand_v, loc_sem.at[0])
    q_load = pltpu.make_async_copy(q_hbm, qall.at[me], loc_sem.at[1])
    p_load = pltpu.make_async_copy(p_hbm, pas, loc_sem.at[2])
    l_load = pltpu.make_async_copy(len_hbm, len_s, loc_sem.at[3])
    c_load.start()
    l_load.start()
    p_load.start()
    q_load.start()
    pl.semaphore_wait(barrier, 3)
    for d in range(2):
        first(d, 0).start()

    c_load.wait()
    across = jnp.broadcast_to(cand_v[...], (number, number))
    down = across.T
    down_owner = lax.div(down, per_owner)
    local_id = down[:, :1] - down_owner[:, :1] * per_owner
    r_at = lax.broadcasted_iota(jnp.int32, (number, number), 0)
    c_at = lax.broadcasted_iota(jnp.int32, (number, number), 1)
    ahead = jnp.where((lax.div(across, per_owner) == down_owner) & (c_at < r_at), 1.0, 0.0)
    slot = down_owner[:, :1].astype(jnp.float32) * float(slots) + jnp.sum(ahead, axis=1, keepdims=True)
    slot_at = lax.broadcasted_iota(jnp.int32, place.shape, 1).astype(jnp.float32)
    spot = slot_at == slot
    line = jnp.max(jnp.where(spot, local_id, 0), axis=0, keepdims=True)
    line = jnp.concatenate([line[:, i * 128:(i + 1) * 128] for i in range(n * slots // 128)], axis=0)
    for d in range(2):
        table[d, me] = line
    place[...] = jnp.where(spot, 1.0, 0.0).astype(place.dtype)
    row_at = lax.broadcasted_iota(jnp.int32, (col, 128), 0) // tok
    lane_at = lax.broadcasted_iota(jnp.int32, (col, 128), 1)
    fold[...] = jnp.where(row_at == lane_at, 1.0, 0.0).astype(fold.dtype)
    for d in range(2):
        table_hop(d, 1, me).start()
    table_share(0, 0, me).start()
    near_out(0).start()
    for k in range(1, pieces):
        for d in range(2):
            first(d, k).start()
        near_out(k).start()
    to_scalar(0, me, 0).start()

    in_tile = lax.broadcasted_iota(jnp.int32, (tile_rows, feature), 0)
    l_load.wait()
    p_load.wait()

    def fill(i, _):
        for j in range(4):
            p = i * 4 + j
            tile = pas[p].astype(jnp.float32)
            tile = jnp.where(in_tile < len_s[p], tile, tile[0:1, :])
            pas[p] = tile.astype(pas.dtype)
        return 0

    lax.fori_loop(0, per_owner // 4, fill, 0)

    def gather_max(slot, d, b, units_of):
        chosen = [wanted[d, b, my_lane + s] for s in range(cap)]
        for u in units_of:
            qs = qall[b, pl.ds(u * col, col), :]
            near = []
            for s in range(cap):
                sim = lax.dot_general(pas[chosen[s]], qs, (((1,), (1,)), ((), ())),
                                      preferred_element_type=jnp.float32)
                near.append(jnp.max(sim, axis=0, keepdims=True))
            if cap < slots:
                near.append(jnp.zeros((slots - cap, col), jnp.float32))
            near = jnp.concatenate(near, axis=0)
            high = near.astype(jnp.bfloat16).astype(jnp.float32)
            both = jnp.concatenate([high, near - high], axis=0).astype(stage.dtype)
            stage[slot, pl.ds(u * 2 * slots, 2 * slots), :] = both

    def add_up(slot, b):
        part = jnp.dot(stage[slot], fold[...], preferred_element_type=jnp.float32)
        total = None
        for u in range(units):
            at_u = u * 2 * slots
            one = part[at_u:at_u + slots] + part[at_u + slots:at_u + 2 * slots]
            if u > 0:
                one = pltpu.roll(one, u * (col // tok), 1)
            total = one if total is None else total + one
        send_buf[b] = total / float(tok)

    def take_tables(s, forward):
        for d in range(2):
            b = origin(d, s, core)
            table_hop(d, s, b).wait_recv()
            if forward is True:
                table_hop(d, s + 1, b).start()
            elif forward is not False:
                @pl.when(forward)
                def _(d=d, b=b):
                    table_hop(d, s + 1, b).start()
            table_share(d, s, b).start()
            to_scalar(d, b, 0).start()

    def own_tables(s):
        for d in range(2):
            to_scalar(d, origin(d, s, core), 0).wait()

    def sib_tables(s):
        for d in range(2):
            b = origin(d, s, 1 - core)
            table_share(d, s, b).wait_recv()
            to_scalar(d, b, 1).start()

    def sib_tables_wait(s):
        for d in range(2):
            to_scalar(d, origin(d, s, 1 - core), 1).wait()

    q_load.wait()
    to_scalar(0, me, 0).wait()
    gather_max(2, 0, me, range(units))
    table_share(0, 0, sib).wait_recv()
    to_scalar(0, sib, 1).start()
    for k in range(pieces):
        near_in(k).wait_recv()
    to_scalar(0, sib, 1).wait()
    gather_max(3, 0, sib, range(units))
    take_tables(1, True)

    def pair(s, k, c, folds=()):
        base = 0 if c is core else 2
        for slot, b in folds:
            add_up(slot, b)
        for d in range(2):
            gather_max(base + d, d, origin(d, s, c), range(*spans[k]))

    def sib_pair(s, k, folds=()):
        if k == 0:
            sib_tables_wait(s)
        for d in range(2):
            share(d, s, k, origin(d, s, 1 - core)).wait_recv()
        pair(s, k, 1 - core, folds)

    def step(s, _):
        opening = s == 1
        old = [jnp.where(opening, me, origin(0, s - 1, 1 - core)),
               jnp.where(opening, sib, origin(1, s - 1, 1 - core))]
        new = [origin(d, s, core) for d in range(2)]
        for k in range(pieces):
            for d in range(2):
                b = new[d]
                hop(d, s, k, b).wait_recv()

                @pl.when(s + 1 < half)
                def _(d=d, k=k, b=b):
                    hop(d, s + 1, k, b).start()
                share(d, s, k, b).start()

            @pl.when(s + 1 == half)
            def _(k=k):
                e = 0 if spans[k][1] <= cut else 1
                d = lax.rem(e + core, 2)
                b = at(pos + (2 * d - 1) * (half - 1), core)
                for u in range(*spans[k]):
                    end_hop(e, u, b).start()
            if k == 0:
                own_tables(s)
                sib_tables(s)
            if k == pieces - 1:
                take_tables(s + 1, s + 2 <= half)
            pair(s, k, core, [(2, old[0]), (3, old[1])] if k == 0 else ())
            if k == 0:
                score_copy(old[1]).start()

                @pl.when(s > 1)
                def _():
                    score_copy(old[0]).start()
            else:
                sib_pair(s, k - 1)
        sib_pair(s, pieces - 1, [(0, new[0]), (1, new[1])])
        for b in new:
            score_copy(b).start()
        return 0

    lax.fori_loop(1, half, step, 0)

    mine, other = at(pos + half, core), at(pos + half, 1 - core)
    own_tables(half)
    sib_tables(half)
    groups = [[t] + ([cut + t] if cut + t < units else []) for t in range(cut)]
    for t, us in enumerate(groups):
        for u in us:
            end_hop(0 if u < cut else 1, u, mine).wait_recv()
            end_share(u, mine).start()
        if t == 0:
            old = [origin(d, half - 1, 1 - core) for d in range(2)]
            for d in range(2):
                add_up(2 + d, old[d])
            gather_max(0, 0, mine, us)
            for b in old:
                score_copy(b).start()
            sib_tables_wait(half)
        else:
            gather_max(0, 0, mine, us)
            for u in groups[t - 1]:
                end_share(u, other).wait_recv()
            if t == cut - 1:
                add_up(0, mine)
            gather_max(2, 0, other, groups[t - 1])
            if t == cut - 1:
                score_copy(mine).start()
    for u in groups[-1]:
        end_share(u, other).wait_recv()
    gather_max(2, 0, other, groups[-1])
    add_up(2, other)
    score_copy(other).start()

    table_share(0, 0, me).wait_send()
    for k in range(pieces):
        near_out(k).wait_send()
        for d in range(2):
            first(d, k).wait_send()
    for d in range(2):
        table_hop(d, 1, me).wait_send()

    def drain(s, _):
        for d in range(2):
            b = origin(d, s, core)
            table_share(d, s, b).wait_send()

            @pl.when(s < half)
            def _(d=d, b=b):
                table_hop(d, s + 1, b).wait_send()
                for k in range(pieces):
                    share(d, s, k, b).wait_send()

            @pl.when(s + 1 < half)
            def _(d=d, b=b):
                for k in range(pieces):
                    hop(d, s + 1, k, b).wait_send()
        return 0

    lax.fori_loop(1, half + 1, drain, 0)
    for u in range(units):
        end_hop(0 if u < cut else 1, u, mine).wait_send()
        end_share(u, mine).wait_send()

    def each(fn):
        def body(o, _):
            fn(lax.rem(me + o, n))
            return 0
        lax.fori_loop(1, n, body, 0)

    each(lambda b: score_copy(b).wait_send())
    each(lambda b: score_in(b).wait_recv())
    got[me] = send_buf[me]
    out_ref[...] = got[...].reshape(out_ref.shape)
    place_ref[...] = place[...]


def finish(got_ref, place_ref, out_ref, best_ref):
    spread = None
    for part in split3(got_ref[...]):
        term = jnp.dot(place_ref[...], part, preferred_element_type=jnp.float32)
        spread = term if spread is None else spread + term
    queries = out_ref.shape[0]
    out_ref[...] = spread.T[:queries]
    best_ref[...] = sort_down(spread).T[:queries, :best_ref.shape[1]]


def local(ways, queries, passages, lengths, candidates):
    n = lax.axis_size("corpus")
    per_owner, tile_rows, feature = passages.shape
    per_device, tok = queries.shape[0], queries.shape[1]
    number = candidates.shape[1]
    rows = per_device * tok
    cap = max(2, 3 * number // (2 * n))
    slots = -(-cap // 8) * 8
    col = pick_tile(rows, tok)
    half = n // 4
    units = rows // col
    cfg = (n, ways, cap, per_owner, tile_rows, rows, feature, tok, col)
    dma = pltpu.SemaphoreType.DMA
    got, place = pl.pallas_call(
        functools.partial(kernel, cfg),
        out_shape=(
            jax.ShapeDtypeStruct((n * slots, 128), jnp.float32),
            jax.ShapeDtypeStruct((number, n * slots), jnp.bfloat16),
        ),
        in_specs=[pl.BlockSpec(memory_space=pl.ANY)] * 4,
        out_specs=(
            pl.BlockSpec(memory_space=pltpu.VMEM),
            pl.BlockSpec(memory_space=pltpu.VMEM),
        ),
        scratch_shapes=[
            pltpu.VMEM((n, rows, feature), queries.dtype),
            pltpu.VMEM(passages.shape, passages.dtype),
            pltpu.VMEM((1, number), jnp.int32),
            pltpu.SMEM((per_owner,), jnp.int32),
            pltpu.VMEM((2, n, n * slots // 128, 128), jnp.int32),
            pltpu.SMEM((2, n, 128), jnp.int32),
            pltpu.VMEM((number, n * slots), jnp.bfloat16),
            pltpu.VMEM((col, 128), jnp.bfloat16),
            pltpu.VMEM((4, 2 * slots * units, col), jnp.bfloat16),
            pltpu.VMEM((n, slots, 128), jnp.float32),
            pltpu.VMEM((n, slots, 128), jnp.float32),
            dma((2, half + 1, 4)), dma((2, half + 1, 4)),
            dma((2, half + 1, 4)), dma((2, half + 1, 4)),
            dma((units,)), dma((units,)),
            dma((4,)), dma((4,)),
            dma((units,)), dma((units,)),
            dma((2, half + 1)), dma((2, half + 1)),
            dma((2, half + 1)), dma((2, half + 1)),
            dma((2, 2)),
            dma((n,)), dma((n,)),
            dma((4,)),
        ],
        compiler_params=pltpu.CompilerParams(
            collective_id=0, has_side_effects=True, vmem_limit_bytes=60 * 2**20),
    )(candidates, lengths, queries.reshape(rows, feature), passages)
    return pl.pallas_call(
        finish,
        out_shape=(
            jax.ShapeDtypeStruct((per_device, number), jnp.float32),
            jax.ShapeDtypeStruct((per_device, TOPK), jnp.float32),
        ),
        in_specs=[pl.BlockSpec(memory_space=pltpu.VMEM)] * 2,
        out_specs=(pl.BlockSpec(memory_space=pltpu.VMEM), pl.BlockSpec(memory_space=pltpu.VMEM)),
    )(got, place)


def solution(mesh):
    ways = 2 if mesh.shape["groups"] == 2 else 1
    return jax.shard_map(
        functools.partial(local, ways),
        mesh=mesh,
        in_specs=(
            P(("groups", "corpus"), None, None),
            P(("groups", "corpus"), None, None),
            P(("groups", "corpus")),
            P(("groups", "corpus"), None),
        ),
        out_specs=(P(("groups", "corpus"), None), P(("groups", "corpus"), None)),
        check_vma=False,
    )
```

time: 56.8 us -> 54.9 us (0.967)
  Pallas kernels: 56 us -> 54.1 us
    pallas_call x1, Pallas kernels: 53.9 us -> 52.1 us  [local(): pl.pallas_call(functools.partial(kernel, cfg), out_shape=(jax.ShapeDtypeS...]
where the time goes in v1:
time: 54.9 us; the launch traced here: 54.8 us
  Pallas kernels  54.1 us (99%)
  between operations  0.64 us (1%)
    pallas_call x1, Pallas kernels, local(): pl.pallas_call(functools.partial(kernel, cfg), out_shape=(jax.ShapeDtypeS...  52.1 us
    pallas_call x1, Pallas kernels, local(): pl.pallas_call(finish, out_shape=(jax.ShapeDtypeStruct((per_device, numbe...  2.08 us

profile of v1, /device:TPU:0, one launch (start us, length us, event | category | flops | bytes accessed | tf_op | source)
XLA Modules:
  0.0 54.8 jit_solution(47458651920940451)
XLA Ops:
  0.6 52.1 %shard_map.59 = (f32[256,128]{1,0:T(8,128)}, bf16[128,256]{1,0:T(8,128)(2,1)}) custom-call(s32[1,128]{1,0:T(1,128)} %cand_hbm.1, s32[128]{0:T(128)} %len_hbm.1, bf16[1792,128]{1,0:T(8,128)(2,1)} %bitcast.1, bf16[128,128,128]{2,1,0:T(8,128)(2,1)} %p_hbm.1), custom_call_target="tpu_custom_call" | custom-call | tf_op jit(solution)/shard_map/pallas_call | solution.py:427
  52.7 2.1 %shard_map.60 = (f32[56,128]{1,0:T(8,128)}, f32[56,100]{1,0:T(8,128)}) custom-call(f32[256,128]{1,0:T(8,128)} %get-tuple-element.4.got_ref, bf16[128,256]{1,0:T(8,128)(2,1)} %get-tuple-element.5.place_ref), custom_call_target="tpu_custom_call" | custom-call | tf_op jit(solution)/shard_map/pallas_call | solution.py:464

commit v2 on v1

--- a/solution.py
+++ b/solution.py
@@ -50,10 +50,9 @@
     return high, mid, low
 
 
-def kernel(cfg, cand_hbm, len_hbm, q_hbm, p_hbm, out_ref, place_ref, qall, pas, cand_v, len_s,
-           table, wanted, place, fold, stage, send_buf, got, q_send, q_recv, sib_send, sib_recv,
-           end_send, end_recv, near_send, near_recv, tail_send, tail_recv, t_send, t_recv,
-           tsib_send, tsib_recv, sm_sem, sc_send, sc_recv, loc_sem):
+def kernel(cfg, cand_hbm, len_hbm, q_hbm, p_hbm, out_ref, best_ref, qall, pas, cand_v, len_s,
+           table, wanted, place, fold, stage, send_buf, got, q_sent, t_sent, sc_sent, q_recv,
+           sib_recv, end_recv, tail_recv, t_recv, tsib_recv, sc_recv, sm_sem, loc_sem):
     n, ways, cap, per_owner, tile_rows, rows, feature, tok, col = cfg
     chips = n // 2
     half = chips // 2
@@ -100,39 +99,42 @@
     def first(d, k):
         cut_k = span_of(*spans[k])
         return remote(q_hbm.at[cut_k, :], qall.at[me, cut_k, :],
-                      q_send.at[d, 1, k], q_recv.at[d, 1, k], toward[d])
+                      q_sent.at[0], q_recv.at[d, 0, k], toward[d])
 
     def hop(d, s, k, b):
         piece = qall.at[b, span_of(*spans[k]), :]
-        return remote(piece, piece, q_send.at[d, s, k], q_recv.at[d, s, k], toward[d])
+        return remote(piece, piece, q_sent.at[0], q_recv.at[d, s - 1, k], toward[d])
 
     def share(d, s, k, b):
         piece = qall.at[b, span_of(*spans[k]), :]
-        return remote(piece, piece, sib_send.at[d, s, k], sib_recv.at[d, s, k], sib)
-
-    def near_out(k):
-        cut_k = span_of(*spans[k])
-        return remote(q_hbm.at[cut_k, :], qall.at[me, cut_k, :],
-                      near_send.at[k], near_recv.at[k], sib)
-
-    def near_in(k):
-        piece = qall.at[sib, span_of(*spans[k]), :]
-        return remote(piece, piece, near_send.at[k], near_recv.at[k], sib)
-
-    def end_hop(e, u, b):
-        d = lax.rem(e + core, 2)
-        piece = qall.at[b, span_of(u, u + 1), :]
-        return remote(piece, piece, end_send.at[u], end_recv.at[u], at(pos + 1 - 2 * d, core))
-
-    def end_share(u, b):
-        piece = qall.at[b, span_of(u, u + 1), :]
-        return remote(piece, piece, tail_send.at[u], tail_recv.at[u], sib)
+        return remote(piece, piece, q_sent.at[0], sib_recv.at[d, s - 1, k], sib)
+
+    def near_out():
+        return remote(q_hbm, qall.at[me], q_sent.at[0], loc_sem.at[4], sib)
+
+    def near_in():
+        return remote(qall.at[sib], qall.at[sib], q_sent.at[0], loc_sem.at[4], sib)
+
+    def end_hop(k, b):
+        d = lax.rem((0 if spans[k][1] <= cut else 1) + core, 2)
+        piece = qall.at[b, span_of(*spans[k]), :]
+        return remote(piece, piece, q_sent.at[0], end_recv.at[k], at(pos + 1 - 2 * d, core))
+
+    def end_share(k, b):
+        piece = qall.at[b, span_of(*spans[k]), :]
+        return remote(piece, piece, q_sent.at[0], tail_recv.at[k], sib)
 
     def table_hop(d, s, b):
-        return remote(table.at[d, b], table.at[d, b], t_send.at[d, s], t_recv.at[d, s], toward[d])
+        return remote(table.at[d, b], table.at[d, b], t_sent.at[0], t_recv.at[s - 1], toward[d])
 
     def table_share(d, s, b):
-        return remote(table.at[d, b], table.at[d, b], tsib_send.at[d, s], tsib_recv.at[d, s], sib)
+        return remote(table.at[d, b], table.at[d, b], t_sent.at[0], tsib_recv.at[s - 1], sib)
+
+    def two_tables(recv):
+        return remote(table.at[:, 0], table.at[:, 0], t_sent.at[0], recv, sib)
+
+    def near_table(b):
+        return remote(table.at[0, b], table.at[0, b], loc_sem.at[6], loc_sem.at[5], sib)
 
     my_row = me * slots // 128
     my_lane = lax.rem(me * slots, 128)
@@ -142,10 +144,11 @@
                                      wanted.at[d, pl.ds(b, 1), :], sm_sem.at[who, d])
 
     def score_copy(b):
-        return remote(send_buf.at[b], got.at[me], sc_send.at[b], sc_recv.at[me], b)
-
-    def score_in(b):
-        return remote(send_buf.at[b], got.at[b], sc_send.at[b], sc_recv.at[b], b)
+        return remote(send_buf.at[b], got.at[me], sc_sent.at[0], sc_recv.at[0], b)
+
+    def all_scores():
+        return remote(send_buf.at[pl.ds(0, n - 1)], got.at[pl.ds(0, n - 1)],
+                      sc_sent.at[0], sc_recv.at[0], sib)
 
     barrier = pltpu.get_barrier_semaphore()
     for peer in (*toward, sib):
@@ -183,12 +186,11 @@
     fold[...] = jnp.where(row_at == lane_at, 1.0, 0.0).astype(fold.dtype)
     for d in range(2):
         table_hop(d, 1, me).start()
-    table_share(0, 0, me).start()
-    near_out(0).start()
+    near_table(me).start()
+    near_out().start()
     for k in range(1, pieces):
         for d in range(2):
             first(d, k).start()
-        near_out(k).start()
     to_scalar(0, me, 0).start()
 
     in_tile = lax.broadcasted_iota(jnp.int32, (tile_rows, feature), 0)
@@ -232,16 +234,14 @@
             total = one if total is None else total + one
         send_buf[b] = total / float(tok)
 
-    def take_tables(s, forward):
+    def take_tables(s):
+        two_tables(t_recv.at[s - 1]).wait_recv()
         for d in range(2):
             b = origin(d, s, core)
-            table_hop(d, s, b).wait_recv()
-            if forward is True:
+
+            @pl.when(s < half)
+            def _(d=d, b=b):
                 table_hop(d, s + 1, b).start()
-            elif forward is not False:
-                @pl.when(forward)
-                def _(d=d, b=b):
-                    table_hop(d, s + 1, b).start()
             table_share(d, s, b).start()
             to_scalar(d, b, 0).start()
 
@@ -250,10 +250,9 @@
             to_scalar(d, origin(d, s, core), 0).wait()
 
     def sib_tables(s):
-        for d in range(2):
-            b = origin(d, s, 1 - core)
-            table_share(d, s, b).wait_recv()
-            to_scalar(d, b, 1).start()
+        two_tables(tsib_recv.at[s - 1]).wait_recv()
+        for d in range(2):
+            to_scalar(d, origin(d, s, 1 - core), 1).start()
 
     def sib_tables_wait(s):
         for d in range(2):
@@ -262,13 +261,12 @@
     q_load.wait()
     to_scalar(0, me, 0).wait()
     gather_max(2, 0, me, range(units))
-    table_share(0, 0, sib).wait_recv()
+    near_table(sib).wait_recv()
     to_scalar(0, sib, 1).start()
-    for k in range(pieces):
-        near_in(k).wait_recv()
+    near_in().wait_recv()
     to_scalar(0, sib, 1).wait()
     gather_max(3, 0, sib, range(units))
-    take_tables(1, True)
+    take_tables(1)
 
     def pair(s, k, c, folds=()):
         base = 0 if c is core else 2
@@ -301,16 +299,13 @@
 
             @pl.when(s + 1 == half)
             def _(k=k):
-                e = 0 if spans[k][1] <= cut else 1
-                d = lax.rem(e + core, 2)
-                b = at(pos + (2 * d - 1) * (half - 1), core)
-                for u in range(*spans[k]):
-                    end_hop(e, u, b).start()
+                d = lax.rem((0 if spans[k][1] <= cut else 1) + core, 2)
+                end_hop(k, at(pos + (2 * d - 1) * (half - 1), core)).start()
             if k == 0:
                 own_tables(s)
                 sib_tables(s)
             if k == pieces - 1:
-                take_tables(s + 1, s + 2 <= half)
+                take_tables(s + 1)
             pair(s, k, core, [(2, old[0]), (3, old[1])] if k == 0 else ())
             if k == 0:
                 score_copy(old[1]).start()
@@ -318,9 +313,7 @@
                 @pl.when(s > 1)
                 def _():
                     score_copy(old[0]).start()
-            else:
-                sib_pair(s, k - 1)
-        sib_pair(s, pieces - 1, [(0, new[0]), (1, new[1])])
+            sib_pair(s, k, [(0, new[0]), (1, new[1])] if k == pieces - 1 else ())
         for b in new:
             score_copy(b).start()
         return 0
@@ -330,81 +323,46 @@
     mine, other = at(pos + half, core), at(pos + half, 1 - core)
     own_tables(half)
     sib_tables(half)
-    groups = [[t] + ([cut + t] if cut + t < units else []) for t in range(cut)]
-    for t, us in enumerate(groups):
-        for u in us:
-            end_hop(0 if u < cut else 1, u, mine).wait_recv()
-            end_share(u, mine).start()
+    early = [k for k in range(pieces) if spans[k][1] <= cut]
+    late = [k for k in range(pieces) if spans[k][1] > cut]
+    groups = [[x[t] for x in (early, late) if t < len(x)] for t in range(max(len(early), len(late)))]
+
+    def units_of(ks):
+        return [u for k in ks for u in range(*spans[k])]
+
+    for t, ks in enumerate(groups):
+        for k in ks:
+            end_hop(k, mine).wait_recv()
+            end_share(k, mine).start()
         if t == 0:
             old = [origin(d, half - 1, 1 - core) for d in range(2)]
             for d in range(2):
                 add_up(2 + d, old[d])
-            gather_max(0, 0, mine, us)
+        gather_max(0, 0, mine, units_of(ks))
+        if t == 0:
             for b in old:
                 score_copy(b).start()
             sib_tables_wait(half)
-        else:
-            gather_max(0, 0, mine, us)
-            for u in groups[t - 1]:
-                end_share(u, other).wait_recv()
-            if t == cut - 1:
-                add_up(0, mine)
-            gather_max(2, 0, other, groups[t - 1])
-            if t == cut - 1:
-                score_copy(mine).start()
-    for u in groups[-1]:
-        end_share(u, other).wait_recv()
-    gather_max(2, 0, other, groups[-1])
+        for k in ks:
+            end_share(k, other).wait_recv()
+        if t == len(groups) - 1:
+            add_up(0, mine)
+        gather_max(2, 0, other, units_of(ks))
+    score_copy(mine).start()
     add_up(2, other)
     score_copy(other).start()
 
-    table_share(0, 0, me).wait_send()
-    for k in range(pieces):
-        near_out(k).wait_send()
-        for d in range(2):
-            first(d, k).wait_send()
-    for d in range(2):
-        table_hop(d, 1, me).wait_send()
-
-    def drain(s, _):
-        for d in range(2):
-            b = origin(d, s, core)
-            table_share(d, s, b).wait_send()
-
-            @pl.when(s < half)
-            def _(d=d, b=b):
-                table_hop(d, s + 1, b).wait_send()
-                for k in range(pieces):
-                    share(d, s, k, b).wait_send()
-
-            @pl.when(s + 1 < half)
-            def _(d=d, b=b):
-                for k in range(pieces):
-                    hop(d, s + 1, k, b).wait_send()
-        return 0
-
-    lax.fori_loop(1, half + 1, drain, 0)
-    for u in range(units):
-        end_hop(0 if u < cut else 1, u, mine).wait_send()
-        end_share(u, mine).wait_send()
-
-    def each(fn):
-        def body(o, _):
-            fn(lax.rem(me + o, n))
-            return 0
-        lax.fori_loop(1, n, body, 0)
-
-    each(lambda b: score_copy(b).wait_send())
-    each(lambda b: score_in(b).wait_recv())
+    remote(qall.at[pl.ds(0, n - 1)], qall.at[pl.ds(0, n - 1)], q_sent.at[0], loc_sem.at[4],
+           sib).wait_send()
+    remote(table.at[:, pl.ds(0, n // 2)], table.at[:, pl.ds(0, n // 2)], t_sent.at[0],
+           loc_sem.at[5], sib).wait_send()
+    near_table(me).wait_send()
+    all_scores().wait_send()
+    all_scores().wait_recv()
     got[me] = send_buf[me]
-    out_ref[...] = got[...].reshape(out_ref.shape)
-    place_ref[...] = place[...]
-
-
-def finish(got_ref, place_ref, out_ref, best_ref):
     spread = None
-    for part in split3(got_ref[...]):
-        term = jnp.dot(place_ref[...], part, preferred_element_type=jnp.float32)
+    for part in split3(got[...].reshape(n * slots, 128)):
+        term = jnp.dot(place[...], part, preferred_element_type=jnp.float32)
         spread = term if spread is None else spread + term
     queries = out_ref.shape[0]
     out_ref[...] = spread.T[:queries]
@@ -424,11 +382,11 @@
     units = rows // col
     cfg = (n, ways, cap, per_owner, tile_rows, rows, feature, tok, col)
     dma = pltpu.SemaphoreType.DMA
-    got, place = pl.pallas_call(
+    return pl.pallas_call(
         functools.partial(kernel, cfg),
         out_shape=(
-            jax.ShapeDtypeStruct((n * slots, 128), jnp.float32),
-            jax.ShapeDtypeStruct((number, n * slots), jnp.bfloat16),
+            pltpu.VMEM((per_device, number), jnp.float32),
+            pltpu.VMEM((per_device, TOPK), jnp.float32),
         ),
         in_specs=[pl.BlockSpec(memory_space=pl.ANY)] * 4,
         out_specs=(
@@ -447,29 +405,17 @@
             pltpu.VMEM((4, 2 * slots * units, col), jnp.bfloat16),
             pltpu.VMEM((n, slots, 128), jnp.float32),
             pltpu.VMEM((n, slots, 128), jnp.float32),
-            dma((2, half + 1, 4)), dma((2, half + 1, 4)),
-            dma((2, half + 1, 4)), dma((2, half + 1, 4)),
-            dma((units,)), dma((units,)),
+            dma((1,)), dma((1,)), dma((1,)),
+            dma((2, half - 1, 4)), dma((2, half - 1, 4)),
             dma((4,)), dma((4,)),
-            dma((units,)), dma((units,)),
-            dma((2, half + 1)), dma((2, half + 1)),
-            dma((2, half + 1)), dma((2, half + 1)),
+            dma((half,)), dma((half,)),
+            dma((1,)),
             dma((2, 2)),
-            dma((n,)), dma((n,)),
-            dma((4,)),
+            dma((7,)),
         ],
         compiler_params=pltpu.CompilerParams(
             collective_id=0, has_side_effects=True, vmem_limit_bytes=60 * 2**20),
     )(candidates, lengths, queries.reshape(rows, feature), passages)
-    return pl.pallas_call(
-        finish,
-        out_shape=(
-            jax.ShapeDtypeStruct((per_device, number), jnp.float32),
-            jax.ShapeDtypeStruct((per_device, TOPK), jnp.float32),
-        ),
-        in_specs=[pl.BlockSpec(memory_space=pltpu.VMEM)] * 2,
-        out_specs=(pl.BlockSpec(memory_space=pltpu.VMEM), pl.BlockSpec(memory_space=pltpu.VMEM)),
-    )(got, place)
 
 
 def solution(mesh):

time: 54.9 us -> 52.4 us (0.954)
  Pallas kernels: 54.1 us -> 50.4 us
  local copies, waits for them, and re-layouts: 0 us -> 1.22 us
    pallas_call x2 -> x1, Pallas kernels: 54.1 us -> 50.4 us  [local(): pl.pallas_call(functools.partial(kernel, cfg), out_shape=(pltpu.VMEM((per...]
    unnamed x0 -> x2, local copies, waits for them, and re-layouts: none -> 1.22 us
where the time goes in v2:
time: 52.4 us; the launch traced here: 52.3 us
  Pallas kernels  50.4 us (96%)
  local copies, waits for them, and re-layouts  1.22 us (2%)
  between operations  0.64 us (1%)
    pallas_call x1, Pallas kernels, local(): pl.pallas_call(functools.partial(kernel, cfg), out_shape=(pltpu.VMEM((per...  50.4 us
    unnamed x2, local copies, waits for them, and re-layouts  1.22 us

profile of v2, /device:TPU:0, one launch (start us, length us, event | category | flops | bytes accessed | tf_op | source)
XLA Modules:
  0.0 52.3 jit_solution(6112602713774930635)
XLA Ops:
  0.6 50.4 %shard_map.59 = (f32[56,128]{1,0:T(8,128)S(1)}, f32[56,100]{1,0:T(8,128)S(1)}) custom-call(s32[1,128]{1,0:T(1,128)} %cand_hbm.1, s32[128]{0:T(128)} %len_hbm.1, bf16[1792,128]{1,0:T(8,128)(2,1)} %bitcast.1, bf16[128,128,128]{2,1,0:T(8,128)(2,1)} %p_hbm.1), custom_call_target="tpu_custom_call" | custom-call | tf_op jit(solution)/shard_map/pallas_call | solution.py:385
  51.0 0.6 %copy.8 = f32[56,128]{1,0:T(8,128)} copy(f32[56,128]{1,0:T(8,128)S(1)} %get-tuple-element.2) | data formatting | bytes 57344
  51.6 0.6 %copy.9 = f32[56,100]{1,0:T(8,128)} copy(f32[56,100]{1,0:T(8,128)S(1)} %get-tuple-element.3) | data formatting | bytes 44800

commit v3 on v2

--- a/solution.py
+++ b/solution.py
@@ -64,6 +64,9 @@
         mid = (lo + hi + 1) // 2
         spans += [(a, b) for a, b in ((lo, mid), (mid, hi)) if b > a]
     pieces = len(spans)
+    early = [k for k in range(pieces) if spans[k][1] <= cut]
+    late = [k for k in range(pieces) if spans[k][1] > cut]
+    order = (early + late, late + early)
     slots = send_buf.shape[1]
     number = cand_hbm.shape[1]
     me = lax.axis_index("corpus")
@@ -83,10 +86,14 @@
         return p * 2 + c
 
     sib = at(pos, 1 - core)
-    toward = (at(pos + 1, core), at(pos - 1, core))
-
-    def origin(d, s, c):
-        return at(pos - s if d == 0 else pos + s, c)
+
+    def sign(e, c):
+        return 1 - 2 * lax.rem(e + c, 2)
+
+    toward = (at(pos + sign(0, core), core), at(pos + sign(1, core), core))
+
+    def origin(e, s, c):
+        return at(pos - sign(e, c) * s, c)
 
     def remote(src, dst, send, recv, peer):
         return pltpu.make_async_remote_copy(
@@ -97,16 +104,16 @@
         return pl.ds(lo * col, (hi - lo) * col)
 
     def first(d, k):
-        cut_k = span_of(*spans[k])
+        cut_k = span_of(*spans[order[d][k]])
         return remote(q_hbm.at[cut_k, :], qall.at[me, cut_k, :],
                       q_sent.at[0], q_recv.at[d, 0, k], toward[d])
 
     def hop(d, s, k, b):
-        piece = qall.at[b, span_of(*spans[k]), :]
+        piece = qall.at[b, span_of(*spans[order[d][k]]), :]
         return remote(piece, piece, q_sent.at[0], q_recv.at[d, s - 1, k], toward[d])
 
     def share(d, s, k, b):
-        piece = qall.at[b, span_of(*spans[k]), :]
+        piece = qall.at[b, span_of(*spans[order[d][k]]), :]
         return remote(piece, piece, q_sent.at[0], sib_recv.at[d, s - 1, k], sib)
 
     def near_out():
@@ -115,14 +122,13 @@
     def near_in():
         return remote(qall.at[sib], qall.at[sib], q_sent.at[0], loc_sem.at[4], sib)
 
-    def end_hop(k, b):
-        d = lax.rem((0 if spans[k][1] <= cut else 1) + core, 2)
-        piece = qall.at[b, span_of(*spans[k]), :]
-        return remote(piece, piece, q_sent.at[0], end_recv.at[k], at(pos + 1 - 2 * d, core))
-
-    def end_share(k, b):
-        piece = qall.at[b, span_of(*spans[k]), :]
-        return remote(piece, piece, q_sent.at[0], tail_recv.at[k], sib)
+    def end_hop(u, b):
+        piece = qall.at[b, span_of(u, u + 1), :]
+        return remote(piece, piece, q_sent.at[0], end_recv.at[u], toward[0 if u < cut else 1])
+
+    def end_share(u, b):
+        piece = qall.at[b, span_of(u, u + 1), :]
+        return remote(piece, piece, q_sent.at[0], tail_recv.at[u], sib)
 
     def table_hop(d, s, b):
         return remote(table.at[d, b], table.at[d, b], t_sent.at[0], t_recv.at[s - 1], toward[d])
@@ -159,11 +165,11 @@
     l_load = pltpu.make_async_copy(len_hbm, len_s, loc_sem.at[3])
     c_load.start()
     l_load.start()
-    p_load.start()
-    q_load.start()
     pl.semaphore_wait(barrier, 3)
     for d in range(2):
         first(d, 0).start()
+    p_load.start()
+    q_load.start()
 
     c_load.wait()
     across = jnp.broadcast_to(cand_v[...], (number, number))
@@ -273,7 +279,7 @@
         for slot, b in folds:
             add_up(slot, b)
         for d in range(2):
-            gather_max(base + d, d, origin(d, s, c), range(*spans[k]))
+            gather_max(base + d, d, origin(d, s, c), range(*spans[order[d][k]]))
 
     def sib_pair(s, k, folds=()):
         if k == 0:
@@ -297,10 +303,15 @@
                     hop(d, s + 1, k, b).start()
                 share(d, s, k, b).start()
 
-            @pl.when(s + 1 == half)
-            def _(k=k):
-                d = lax.rem((0 if spans[k][1] <= cut else 1) + core, 2)
-                end_hop(k, at(pos + (2 * d - 1) * (half - 1), core)).start()
+            ends = [(d, order[d][k]) for d in range(2)
+                    if order[d][k] in (early, late)[d]]
+            if ends:
+                @pl.when(s + 1 == half)
+                def _(ends=ends):
+                    for j in range(2):
+                        for d, p in ends:
+                            if spans[p][0] + j < spans[p][1]:
+                                end_hop(spans[p][0] + j, new[d]).start()
             if k == 0:
                 own_tables(s)
                 sib_tables(s)
@@ -323,32 +334,30 @@
     mine, other = at(pos + half, core), at(pos + half, 1 - core)
     own_tables(half)
     sib_tables(half)
-    early = [k for k in range(pieces) if spans[k][1] <= cut]
-    late = [k for k in range(pieces) if spans[k][1] > cut]
-    groups = [[x[t] for x in (early, late) if t < len(x)] for t in range(max(len(early), len(late)))]
-
-    def units_of(ks):
-        return [u for k in ks for u in range(*spans[k])]
-
-    for t, ks in enumerate(groups):
-        for k in ks:
-            end_hop(k, mine).wait_recv()
-            end_share(k, mine).start()
+    groups = [[t] + ([cut + t] if cut + t < units else []) for t in range(cut)]
+    for t, us in enumerate(groups):
+        for u in us:
+            end_hop(u, mine).wait_recv()
+            end_share(u, mine).start()
         if t == 0:
             old = [origin(d, half - 1, 1 - core) for d in range(2)]
             for d in range(2):
                 add_up(2 + d, old[d])
-        gather_max(0, 0, mine, units_of(ks))
+        gather_max(0, 0, mine, us)
         if t == 0:
             for b in old:
                 score_copy(b).start()
             sib_tables_wait(half)
-        for k in ks:
-            end_share(k, other).wait_recv()
-        if t == len(groups) - 1:
-            add_up(0, mine)
-        gather_max(2, 0, other, units_of(ks))
+        else:
+            for u in groups[t - 1]:
+                end_share(u, other).wait_recv()
+            if t == cut - 1:
+                add_up(0, mine)
+            gather_max(2, 0, other, groups[t - 1])
     score_copy(mine).start()
+    for u in groups[-1]:
+        end_share(u, other).wait_recv()
+    gather_max(2, 0, other, groups[-1])
     add_up(2, other)
     score_copy(other).start()
 
@@ -369,6 +378,15 @@
     best_ref[...] = sort_down(spread).T[:queries, :best_ref.shape[1]]
 
 
+def hand_out(scores_ref, best_ref, scores_hbm, best_hbm, sem):
+    moves = [pltpu.make_async_copy(scores_ref, scores_hbm, sem.at[0]),
+             pltpu.make_async_copy(best_ref, best_hbm, sem.at[1])]
+    for move in moves:
+        move.start()
+    for move in moves:
+        move.wait()
+
+
 def local(ways, queries, passages, lengths, candidates):
     n = lax.axis_size("corpus")
     per_owner, tile_rows, feature = passages.shape
@@ -382,7 +400,7 @@
     units = rows // col
     cfg = (n, ways, cap, per_owner, tile_rows, rows, feature, tok, col)
     dma = pltpu.SemaphoreType.DMA
-    return pl.pallas_call(
+    scores, best = pl.pallas_call(
         functools.partial(kernel, cfg),
         out_shape=(
             pltpu.VMEM((per_device, number), jnp.float32),
@@ -407,7 +425,7 @@
             pltpu.VMEM((n, slots, 128), jnp.float32),
             dma((1,)), dma((1,)), dma((1,)),
             dma((2, half - 1, 4)), dma((2, half - 1, 4)),
-            dma((4,)), dma((4,)),
+            dma((units,)), dma((units,)),
             dma((half,)), dma((half,)),
             dma((1,)),
             dma((2, 2)),
@@ -416,6 +434,18 @@
         compiler_params=pltpu.CompilerParams(
             collective_id=0, has_side_effects=True, vmem_limit_bytes=60 * 2**20),
     )(candidates, lengths, queries.reshape(rows, feature), passages)
+    scores = pltpu.with_memory_space_constraint(scores, pltpu.VMEM)
+    best = pltpu.with_memory_space_constraint(best, pltpu.VMEM)
+    return pl.pallas_call(
+        hand_out,
+        out_shape=(
+            jax.ShapeDtypeStruct((per_device, number), jnp.float32),
+            jax.ShapeDtypeStruct((per_device, TOPK), jnp.float32),
+        ),
+        in_specs=[pl.BlockSpec(memory_space=pltpu.VMEM)] * 2,
+        out_specs=(pl.BlockSpec(memory_space=pl.ANY), pl.BlockSpec(memory_space=pl.ANY)),
+        scratch_shapes=[dma((2,))],
+    )(scores, best)
 
 
 def solution(mesh):

time: 52.4 us -> 51.8 us (0.989)
  local copies, waits for them, and re-layouts: 1.22 us -> 0 us
    unnamed x2 -> x0, local copies, waits for them, and re-layouts: 1.22 us -> none
    pallas_call x0 -> x1, Pallas kernels: none -> 0.64 us  [local(): pl.pallas_call(hand_out, out_shape=(jax.ShapeDtypeStruct((per_device, num...]
where the time goes in v3:
time: 51.8 us; the launch traced here: 51.6 us
  Pallas kernels  50.9 us (98%)
  between operations  0.8 us (2%)
    pallas_call x1, Pallas kernels, local(): pl.pallas_call(functools.partial(kernel, cfg), out_shape=(pltpu.VMEM((per...  50.2 us

profile of v3, /device:TPU:0, one launch (start us, length us, event | category | flops | bytes accessed | tf_op | source)
XLA Modules:
  0.0 51.6 jit_solution(13029802886471414524)
XLA Ops:
  0.6 50.2 %shard_map.59 = (f32[56,128]{1,0:T(8,128)S(1)}, f32[56,100]{1,0:T(8,128)S(1)}) custom-call(s32[1,128]{1,0:T(1,128)} %cand_hbm.1, s32[128]{0:T(128)} %len_hbm.1, bf16[1792,128]{1,0:T(8,128)(2,1)} %bitcast.1, bf16[128,128,128]{2,1,0:T(8,128)(2,1)} %p_hbm.1), custom_call_target="tpu_custom_call" | custom-call | tf_op jit(solution)/shard_map/pallas_call | solution.py:403
  50.9 0.6 %shard_map.60 = (f32[56,128]{1,0:T(8,128)}, f32[56,100]{1,0:T(8,128)}) custom-call(f32[56,128]{1,0:T(8,128)S(1)} %get-tuple-element.4.scores_ref, f32[56,100]{1,0:T(8,128)S(1)} %get-tuple-element.5.best_ref), custom_call_target="tpu_custom_call" | custom-call | tf_op jit(solution)/shard_map/pallas_call | solution.py:439

commit v4 on v3

--- a/solution.py
+++ b/solution.py
@@ -114,7 +114,7 @@
 
     def share(d, s, k, b):
         piece = qall.at[b, span_of(*spans[order[d][k]]), :]
-        return remote(piece, piece, q_sent.at[0], sib_recv.at[d, s - 1, k], sib)
+        return remote(piece, piece, q_sent.at[0], sib_recv.at[s - 1, k], sib)
 
     def near_out():
         return remote(q_hbm, qall.at[me], q_sent.at[0], loc_sem.at[4], sib)
@@ -122,13 +122,17 @@
     def near_in():
         return remote(qall.at[sib], qall.at[sib], q_sent.at[0], loc_sem.at[4], sib)
 
-    def end_hop(u, b):
-        piece = qall.at[b, span_of(u, u + 1), :]
-        return remote(piece, piece, q_sent.at[0], end_recv.at[u], toward[0 if u < cut else 1])
-
-    def end_share(u, b):
-        piece = qall.at[b, span_of(u, u + 1), :]
-        return remote(piece, piece, q_sent.at[0], tail_recv.at[u], sib)
+    def end_hop(k, b):
+        piece = qall.at[b, span_of(*spans[k]), :]
+        return remote(piece, piece, q_sent.at[0], end_recv.at[k], toward[0 if k in early else 1])
+
+    def end_share(t, k, b):
+        piece = qall.at[b, span_of(*spans[k]), :]
+        return remote(piece, piece, q_sent.at[0], tail_recv.at[t], sib)
+
+    def so_many(count, recv):
+        piece = qall.at[0, span_of(0, count), :]
+        return remote(piece, piece, q_sent.at[0], recv, sib)
 
     def table_hop(d, s, b):
         return remote(table.at[d, b], table.at[d, b], t_sent.at[0], t_recv.at[s - 1], toward[d])
@@ -284,8 +288,8 @@
     def sib_pair(s, k, folds=()):
         if k == 0:
             sib_tables_wait(s)
-        for d in range(2):
-            share(d, s, k, origin(d, s, 1 - core)).wait_recv()
+        so_many(sum(spans[order[d][k]][1] - spans[order[d][k]][0] for d in range(2)),
+                sib_recv.at[s - 1, k]).wait_recv()
         pair(s, k, 1 - core, folds)
 
     def step(s, _):
@@ -308,10 +312,8 @@
             if ends:
                 @pl.when(s + 1 == half)
                 def _(ends=ends):
-                    for j in range(2):
-                        for d, p in ends:
-                            if spans[p][0] + j < spans[p][1]:
-                                end_hop(spans[p][0] + j, new[d]).start()
+                    for d, p in ends:
+                        end_hop(p, new[d]).start()
             if k == 0:
                 own_tables(s)
                 sib_tables(s)
@@ -334,13 +336,14 @@
     mine, other = at(pos + half, core), at(pos + half, 1 - core)
     own_tables(half)
     sib_tables(half)
-    groups = [[t] + ([cut + t] if cut + t < units else []) for t in range(cut)]
-    for t, us in enumerate(groups):
-        for u in us:
-            end_hop(u, mine).wait_recv()
-            end_share(u, mine).start()
+    groups = [[x[t] for x in (early, late) if t < len(x)] for t in range(max(len(early), len(late)))]
+    old = [origin(d, half - 1, 1 - core) for d in range(2)]
+    for t, ks in enumerate(groups):
+        us = [u for k in ks for u in range(*spans[k])]
+        for k in ks:
+            end_hop(k, mine).wait_recv()
+            end_share(t, k, mine).start()
         if t == 0:
-            old = [origin(d, half - 1, 1 - core) for d in range(2)]
             for d in range(2):
                 add_up(2 + d, old[d])
         gather_max(0, 0, mine, us)
@@ -348,16 +351,11 @@
             for b in old:
                 score_copy(b).start()
             sib_tables_wait(half)
-        else:
-            for u in groups[t - 1]:
-                end_share(u, other).wait_recv()
-            if t == cut - 1:
-                add_up(0, mine)
-            gather_max(2, 0, other, groups[t - 1])
+        so_many(len(us), tail_recv.at[t]).wait_recv()
+        if t == len(groups) - 1:
+            add_up(0, mine)
+        gather_max(2, 0, other, us)
     score_copy(mine).start()
-    for u in groups[-1]:
-        end_share(u, other).wait_recv()
-    gather_max(2, 0, other, groups[-1])
     add_up(2, other)
     score_copy(other).start()
 
@@ -424,8 +422,8 @@
             pltpu.VMEM((n, slots, 128), jnp.float32),
             pltpu.VMEM((n, slots, 128), jnp.float32),
             dma((1,)), dma((1,)), dma((1,)),
-            dma((2, half - 1, 4)), dma((2, half - 1, 4)),
-            dma((units,)), dma((units,)),
+            dma((2, half - 1, 4)), dma((half - 1, 4)),
+            dma((4,)), dma((2,)),
             dma((half,)), dma((half,)),
             dma((1,)),
             dma((2, 2)),

time: 51.8 us -> 51.7 us (level)
  no operation moved by 1% of the time
where the time goes in v4:
time: 51.7 us; the launch traced here: 51.6 us
  Pallas kernels  50.8 us (98%)
  between operations  0.8 us (2%)
    pallas_call x1, Pallas kernels, local(): pl.pallas_call(functools.partial(kernel, cfg), out_shape=(pltpu.VMEM((per...  50.1 us

profile of v4, /device:TPU:0, one launch (start us, length us, event | category | flops | bytes accessed | tf_op | source)
XLA Modules:
  0.0 51.6 jit_solution(2303808770996605372)
XLA Ops:
  0.6 50.1 %shard_map.59 = (f32[56,128]{1,0:T(8,128)S(1)}, f32[56,100]{1,0:T(8,128)S(1)}) custom-call(s32[1,128]{1,0:T(1,128)} %cand_hbm.1, s32[128]{0:T(128)} %len_hbm.1, bf16[1792,128]{1,0:T(8,128)(2,1)} %bitcast.1, bf16[128,128,128]{2,1,0:T(8,128)(2,1)} %p_hbm.1), custom_call_target="tpu_custom_call" | custom-call | tf_op jit(solution)/shard_map/pallas_call | solution.py:401
  50.8 0.6 %shard_map.60 = (f32[56,128]{1,0:T(8,128)}, f32[56,100]{1,0:T(8,128)}) custom-call(f32[56,128]{1,0:T(8,128)S(1)} %get-tuple-element.4.scores_ref, f32[56,100]{1,0:T(8,128)S(1)} %get-tuple-element.5.best_ref), custom_call_target="tpu_custom_call" | custom-call | tf_op jit(solution)/shard_map/pallas_call | solution.py:437

commit v5 on v4

--- a/solution.py
+++ b/solution.py
@@ -59,14 +59,11 @@
     depth = chips // ways
     units = rows // col
     cut = (units + 1) // 2
-    spans = []
-    for lo, hi in ((0, cut), (cut, units)):
-        mid = (lo + hi + 1) // 2
-        spans += [(a, b) for a, b in ((lo, mid), (mid, hi)) if b > a]
+    first_mid, second_mid = (cut + 1) // 2, (cut + units + 1) // 2
+    bits = [(0, first_mid), (first_mid, cut), (cut, second_mid), (second_mid, units)]
+    spans = [(0, first_mid), (first_mid, cut), (cut, units)]
     pieces = len(spans)
-    early = [k for k in range(pieces) if spans[k][1] <= cut]
-    late = [k for k in range(pieces) if spans[k][1] > cut]
-    order = (early + late, late + early)
+    order = ((0, 1, 2), (2, 0, 1))
     slots = send_buf.shape[1]
     number = cand_hbm.shape[1]
     me = lax.axis_index("corpus")
@@ -123,11 +120,11 @@
         return remote(qall.at[sib], qall.at[sib], q_sent.at[0], loc_sem.at[4], sib)
 
     def end_hop(k, b):
-        piece = qall.at[b, span_of(*spans[k]), :]
-        return remote(piece, piece, q_sent.at[0], end_recv.at[k], toward[0 if k in early else 1])
+        piece = qall.at[b, span_of(*bits[k]), :]
+        return remote(piece, piece, q_sent.at[0], end_recv.at[k], toward[k // 2])
 
     def end_share(t, k, b):
-        piece = qall.at[b, span_of(*spans[k]), :]
+        piece = qall.at[b, span_of(*bits[k]), :]
         return remote(piece, piece, q_sent.at[0], tail_recv.at[t], sib)
 
     def so_many(count, recv):
@@ -286,11 +283,14 @@
             gather_max(base + d, d, origin(d, s, c), range(*spans[order[d][k]]))
 
     def sib_pair(s, k, folds=()):
+        for slot, b in folds:
+            add_up(slot, b)
+            score_copy(b).start()
         if k == 0:
             sib_tables_wait(s)
         so_many(sum(spans[order[d][k]][1] - spans[order[d][k]][0] for d in range(2)),
                 sib_recv.at[s - 1, k]).wait_recv()
-        pair(s, k, 1 - core, folds)
+        pair(s, k, 1 - core)
 
     def step(s, _):
         opening = s == 1
@@ -307,12 +307,12 @@
                     hop(d, s + 1, k, b).start()
                 share(d, s, k, b).start()
 
-            ends = [(d, order[d][k]) for d in range(2)
-                    if order[d][k] in (early, late)[d]]
+            ends = [(p, d) for d in range(2) for p in (2 * d, 2 * d + 1)
+                    if spans[order[d][k]][0] <= bits[p][0] and bits[p][1] <= spans[order[d][k]][1]]
             if ends:
                 @pl.when(s + 1 == half)
                 def _(ends=ends):
-                    for d, p in ends:
+                    for p, d in ends:
                         end_hop(p, new[d]).start()
             if k == 0:
                 own_tables(s)
@@ -327,8 +327,6 @@
                 def _():
                     score_copy(old[0]).start()
             sib_pair(s, k, [(0, new[0]), (1, new[1])] if k == pieces - 1 else ())
-        for b in new:
-            score_copy(b).start()
         return 0
 
     lax.fori_loop(1, half, step, 0)
@@ -336,26 +334,24 @@
     mine, other = at(pos + half, core), at(pos + half, 1 - core)
     own_tables(half)
     sib_tables(half)
-    groups = [[x[t] for x in (early, late) if t < len(x)] for t in range(max(len(early), len(late)))]
+    groups = ((0, 2), (1, 3))
     old = [origin(d, half - 1, 1 - core) for d in range(2)]
     for t, ks in enumerate(groups):
-        us = [u for k in ks for u in range(*spans[k])]
+        us = [u for k in ks for u in range(*bits[k])]
         for k in ks:
             end_hop(k, mine).wait_recv()
             end_share(t, k, mine).start()
+        gather_max(0, 0, mine, us)
         if t == 0:
             for d in range(2):
                 add_up(2 + d, old[d])
-        gather_max(0, 0, mine, us)
-        if t == 0:
-            for b in old:
-                score_copy(b).start()
+                score_copy(old[d]).start()
             sib_tables_wait(half)
-        so_many(len(us), tail_recv.at[t]).wait_recv()
         if t == len(groups) - 1:
             add_up(0, mine)
+            score_copy(mine).start()
+        so_many(len(us), tail_recv.at[t]).wait_recv()
         gather_max(2, 0, other, us)
-    score_copy(mine).start()
     add_up(2, other)
     score_copy(other).start()
 
@@ -422,7 +418,7 @@
             pltpu.VMEM((n, slots, 128), jnp.float32),
             pltpu.VMEM((n, slots, 128), jnp.float32),
             dma((1,)), dma((1,)), dma((1,)),
-            dma((2, half - 1, 4)), dma((half - 1, 4)),
+            dma((2, half - 1, 3)), dma((half - 1, 3)),
             dma((4,)), dma((2,)),
             dma((half,)), dma((half,)),
             dma((1,)),

time: 51.7 us -> 51.5 us (level)
  no operation moved by 1% of the time
where the time goes in v5:
time: 51.5 us; the launch traced here: 51.4 us
  Pallas kernels  50.6 us (98%)
  between operations  0.8 us (2%)
    pallas_call x1, Pallas kernels, local(): pl.pallas_call(functools.partial(kernel, cfg), out_shape=(pltpu.VMEM((per...  49.9 us

profile of v5, /device:TPU:0, one launch (start us, length us, event | category | flops | bytes accessed | tf_op | source)
XLA Modules:
  0.0 51.4 jit_solution(14097400114464372669)
XLA Ops:
  0.6 49.9 %shard_map.59 = (f32[56,128]{1,0:T(8,128)S(1)}, f32[56,100]{1,0:T(8,128)S(1)}) custom-call(s32[1,128]{1,0:T(1,128)} %cand_hbm.1, s32[128]{0:T(128)} %len_hbm.1, bf16[1792,128]{1,0:T(8,128)(2,1)} %bitcast.1, bf16[128,128,128]{2,1,0:T(8,128)(2,1)} %p_hbm.1), custom_call_target="tpu_custom_call" | custom-call | tf_op jit(solution)/shard_map/pallas_call | solution.py:397
  50.6 0.6 %shard_map.60 = (f32[56,128]{1,0:T(8,128)}, f32[56,100]{1,0:T(8,128)}) custom-call(f32[56,128]{1,0:T(8,128)S(1)} %get-tuple-element.4.scores_ref, f32[56,100]{1,0:T(8,128)S(1)} %get-tuple-element.5.best_ref), custom_call_target="tpu_custom_call" | custom-call | tf_op jit(solution)/shard_map/pallas_call | solution.py:433

commit v6 on v5

--- a/solution.py
+++ b/solution.py
@@ -102,7 +102,7 @@
 
     def first(d, k):
         cut_k = span_of(*spans[order[d][k]])
-        return remote(q_hbm.at[cut_k, :], qall.at[me, cut_k, :],
+        return remote(qall.at[me, cut_k, :], qall.at[me, cut_k, :],
                       q_sent.at[0], q_recv.at[d, 0, k], toward[d])
 
     def hop(d, s, k, b):
@@ -114,7 +114,7 @@
         return remote(piece, piece, q_sent.at[0], sib_recv.at[s - 1, k], sib)
 
     def near_out():
-        return remote(q_hbm, qall.at[me], q_sent.at[0], loc_sem.at[4], sib)
+        return remote(qall.at[me], qall.at[me], q_sent.at[0], loc_sem.at[4], sib)
 
     def near_in():
         return remote(qall.at[sib], qall.at[sib], q_sent.at[0], loc_sem.at[4], sib)
@@ -166,11 +166,12 @@
     l_load = pltpu.make_async_copy(len_hbm, len_s, loc_sem.at[3])
     c_load.start()
     l_load.start()
+    q_load.start()
     pl.semaphore_wait(barrier, 3)
+    q_load.wait()
     for d in range(2):
         first(d, 0).start()
     p_load.start()
-    q_load.start()
 
     c_load.wait()
     across = jnp.broadcast_to(cand_v[...], (number, number))
@@ -265,7 +266,6 @@
         for d in range(2):
             to_scalar(d, origin(d, s, 1 - core), 1).wait()
 
-    q_load.wait()
     to_scalar(0, me, 0).wait()
     gather_max(2, 0, me, range(units))
     near_table(sib).wait_recv()

time: 51.5 us -> 51.3 us (level)
  no operation moved by 1% of the time
where the time goes in v6:
time: 51.3 us; the launch traced here: 51.2 us
  Pallas kernels  50.4 us (98%)
  between operations  0.8 us (2%)
    pallas_call x1, Pallas kernels, local(): pl.pallas_call(functools.partial(kernel, cfg), out_shape=(pltpu.VMEM((per...  49.7 us

profile of v6, /device:TPU:0, one launch (start us, length us, event | category | flops | bytes accessed | tf_op | source)
XLA Modules:
  0.0 51.2 jit_solution(10008048729767215853)
XLA Ops:
  0.6 49.7 %shard_map.59 = (f32[56,128]{1,0:T(8,128)S(1)}, f32[56,100]{1,0:T(8,128)S(1)}) custom-call(s32[1,128]{1,0:T(1,128)} %cand_hbm.1, s32[128]{0:T(128)} %len_hbm.1, bf16[1792,128]{1,0:T(8,128)(2,1)} %bitcast.1, bf16[128,128,128]{2,1,0:T(8,128)(2,1)} %p_hbm.1), custom_call_target="tpu_custom_call" | custom-call | tf_op jit(solution)/shard_map/pallas_call | solution.py:397
  50.4 0.6 %shard_map.60 = (f32[56,128]{1,0:T(8,128)}, f32[56,100]{1,0:T(8,128)}) custom-call(f32[56,128]{1,0:T(8,128)S(1)} %get-tuple-element.4.scores_ref, f32[56,100]{1,0:T(8,128)S(1)} %get-tuple-element.5.best_ref), custom_call_target="tpu_custom_call" | custom-call | tf_op jit(solution)/shard_map/pallas_call | solution.py:433
